TPU v7x, 32 devices: a whole 2x2x4 slice. The times are simulated.
32 devices in a mesh: shot: 2 (over y), gx: 4 (over z), gy: 4 (over x, core).
Axes of the slice: x: 2, y: 2, z: 4, core: 2. Of those that a mesh axis runs over, the one named last changes fastest.
Arguments:
- source_prev: float32 [64, 32, 320], P(('shot', 'gx'), 'gy'), parts along dimension 0, may hold values from -0.6 to 0.6
- source_now: float32 [64, 32, 320], P(('shot', 'gx'), 'gy'), parts along dimension 0, may hold values from -0.6 to 0.6
- receiver_prev: float32 [64, 32, 320], P(('shot', 'gx'), 'gy'), parts along dimension 0, may hold values from -6 to 6
- receiver_now: float32 [64, 32, 320], P(('shot', 'gx'), 'gy'), parts along dimension 0, may hold values from -6 to 6
- speed_squared: float32 [64, 32, 320], P(('shot', 'gx'), 'gy'), parts along dimension 0, may hold values from 0.05 to 0.18
- wavelet: float32 [20], P('shot'), parts along dimension 0, may hold values from -40 to 40
- source_cell: int32 [2], P('shot'), parts along dimension 0, may hold values from 0 to 327679
- traces: float32 [20, 1024], P('shot', ('gx', 'gy')), parts along dimension 0, may hold values from -18 to 18
- receiver_cells: int32 [2, 1024], P('shot', ('gx', 'gy')), parts along dimension 0, may hold values from 0 to 1023
- plan: int32 [8], P('shot'), parts along dimension 0, may hold values from 0 to 9, as said below
- stored_snapshots: bfloat16 [8, 32, 32, 320], P('shot', 'gx', 'gy'), parts along dimension 0, may hold values from -6 to 6
- image_before: float32 [64, 32, 320], P(('shot', 'gx'), 'gy'), parts along dimension 0, may hold values from -6 to 6
Outputs:
- new_source_prev: float32 [64, 32, 320], P(('shot', 'gx'), 'gy'), parts along dimension 0
- new_source_now: float32 [64, 32, 320], P(('shot', 'gx'), 'gy'), parts along dimension 0
- new_receiver_prev: float32 [64, 32, 320], P(('shot', 'gx'), 'gy'), parts along dimension 0
- new_receiver_now: float32 [64, 32, 320], P(('shot', 'gx'), 'gy'), parts along dimension 0
- snapshots: bfloat16 [8, 32, 32, 320], P('shot', 'gx', 'gy'), parts along dimension 0
- image: float32 [64, 32, 320], P(('shot', 'gx'), 'gy'), parts along dimension 0
There are 2 independent parts, one for each index of `shot`. A program takes and returns all parts, laid end to end along the dimension named above; each array names one. Nothing has to cross between parts.
Inputs may be any that keep to these rules, and one draw needn't show every extreme that they name: `plan`: 4 different steps in increasing order; the first is 0 and the last is 9.
All inputs are finite; a program needn't handle non-finite values.
Results may differ from a plain program's by a relative error of at most 0.001.
Values sent between devices are 32-bit elements; how exact they have to be, the bound alone decides.
A program may use at most 64 MiB of HBM per device.

v0:
```python
import jax
import jax.numpy as jnp
from jax import lax
from jax.sharding import PartitionSpec as P

STENCIL_COEFFS = (-205.0 / 72.0, 8.0 / 5.0, -1.0 / 5.0, 8.0 / 315.0, -1.0 / 560.0)


def with_halo(block, sides, width):
    for axis, dim in sides:
        count = lax.axis_size(axis)
        forward = [(i, i + 1) for i in range(count - 1)]
        backward = [(target, source) for source, target in forward]
        low = lax.ppermute(
            lax.slice_in_dim(block, block.shape[dim] - width, None, axis=dim), axis, forward
        )
        high = lax.ppermute(lax.slice_in_dim(block, 0, width, axis=dim), axis, backward)
        block = jnp.concatenate([low, block, high], axis=dim)
    return block


def stencil(padded):
    span_x = padded.shape[0] - 8
    span_y = padded.shape[1] - 8
    depth_cells = padded.shape[2]
    deepened = jnp.pad(padded, ((0, 0), (0, 0), (4, 4)))

    def window(shift_x, shift_y, shift_z):
        return deepened[
            4 + shift_x : 4 + shift_x + span_x,
            4 + shift_y : 4 + shift_y + span_y,
            4 + shift_z : 4 + shift_z + depth_cells,
        ]

    summed = 3.0 * STENCIL_COEFFS[0] * window(0, 0, 0)
    for distance in range(1, 5):
        neighbours = window(distance, 0, 0) + window(-distance, 0, 0)
        neighbours = neighbours + window(0, distance, 0) + window(0, -distance, 0)
        neighbours = neighbours + window(0, 0, distance) + window(0, 0, -distance)
        summed = summed + STENCIL_COEFFS[distance] * neighbours
    return summed


def body(
    source_prev,
    source_now,
    receiver_prev,
    receiver_now,
    speed_squared,
    wavelet,
    source_cell,
    traces,
    receiver_cells,
    plan,
    stored_snapshots,
    image_before,
):
    block_x, block_y, depth_cells = source_now.shape
    grid_y = block_y * lax.axis_size("gy")
    start_x = lax.axis_index("gx") * block_x
    start_y = lax.axis_index("gy") * block_y
    total_steps = wavelet.shape[0]
    slot_count = plan.shape[0]
    border = 0
    span_x = block_x + 2 * border
    span_y = block_y + 2 * border
    plane_cells = span_x * span_y
    values = lax.all_gather(traces, ("gx", "gy"), axis=1, tiled=True)
    cell_ids = lax.all_gather(receiver_cells, ("gx", "gy"), axis=1, tiled=True)
    cell_ids = cell_ids[0]
    local_x = cell_ids // grid_y - (start_x - border)
    local_y = cell_ids % grid_y - (start_y - border)
    in_block = (local_x >= 0) & (local_x < span_x) & (local_y >= 0) & (local_y < span_y)
    local_cell = jnp.where(in_block, local_x * span_y + local_y, plane_cells)
    injected = (
        jnp.zeros((total_steps, plane_cells), jnp.float32)
        .at[:, local_cell]
        .add(values, mode="drop")
    )
    injected = injected.reshape(total_steps, span_x, span_y)
    snapshots = jnp.zeros(stored_snapshots.shape, jnp.bfloat16)
    imaged = image_before
    along_x = start_x - 0 + lax.broadcasted_iota(jnp.int32, (block_x + 2 * 0, 1, 1), 0)
    along_y = start_y - 0 + lax.broadcasted_iota(jnp.int32, (1, block_y + 2 * 0, 1), 1)
    along_x, along_y = (along_x, along_y)
    along_z = lax.broadcasted_iota(jnp.int32, (1, 1, depth_cells), 2)
    cell_id = source_cell[0]
    matches = (along_x == cell_id // (grid_y * depth_cells)) & (
        along_y == cell_id // depth_cells % grid_y
    )
    matches = matches & (along_z == cell_id % depth_cells)
    source_core = matches.astype(jnp.float32)
    source_before, source_field = (source_prev, source_now)
    receiver_before, receiver_field = (receiver_prev, receiver_now)
    for step_index in range(total_steps):
        back_time = total_steps - 1 - step_index
        padded = with_halo(jnp.stack([source_field, receiver_field]), (("gx", 1), ("gy", 2)), 4)
        source_spread = stencil(padded[0]) + wavelet[step_index] * source_core
        receiver_spread = stencil(padded[1]).at[:, :, 0].add(injected[back_time])
        source_latest = 2.0 * source_field - source_before + speed_squared * source_spread
        receiver_latest = 2.0 * receiver_field - receiver_before + speed_squared * receiver_spread
        source_before, source_field = (source_field, source_latest)
        receiver_before, receiver_field = (receiver_field, receiver_latest)
        record_matches = plan == step_index
        snapshots = jnp.where(
            record_matches[:, None, None, None], source_field.astype(jnp.bfloat16)[None], snapshots
        )
        correlate_matches = plan == back_time
        slot_index = jnp.sum(
            jnp.where(correlate_matches, jnp.arange(slot_count, dtype=jnp.int32), 0)
        )
        present = jnp.any(correlate_matches)
        snapshot = lax.dynamic_index_in_dim(stored_snapshots, slot_index, 0, keepdims=False).astype(
            jnp.float32
        )
        imaged = imaged + jnp.where(present, snapshot * receiver_field, 0.0)
    source_last, source_final = (source_before, source_field)
    previous, current = (receiver_before, receiver_field)
    return (source_last, source_final, previous, current, snapshots, imaged)


def solution(mesh):
    placed = (
        P(("shot", "gx"), "gy", None),
        P(("shot", "gx"), "gy", None),
        P(("shot", "gx"), "gy", None),
        P(("shot", "gx"), "gy", None),
        P(("shot", "gx"), "gy", None),
        P("shot"),
        P("shot"),
        P("shot", ("gx", "gy")),
        P("shot", ("gx", "gy")),
        P("shot"),
        P("shot", "gx", "gy", None),
        P(("shot", "gx"), "gy", None),
    )
    return jax.shard_map(
        body,
        mesh=mesh,
        in_specs=placed,
        out_specs=(
            P(("shot", "gx"), "gy", None),
            P(("shot", "gx"), "gy", None),
            P(("shot", "gx"), "gy", None),
            P(("shot", "gx"), "gy", None),
            P("shot", "gx", "gy", None),
            P(("shot", "gx"), "gy", None),
        ),
        check_vma=False,
    )
```

profile of v0, /device:TPU:18, one launch (start us, length us, event | category | flops | bytes accessed | tf_op | source)
XLA Modules:
  0.0 254.4 jit_solution(9579591347282151355)
XLA Ops:
  1.6 2.5 collective-permute-start.1
  4.1 3.5 %collective-permute-start = (f32[2,4,8,320]{3,2,1,0:T(8,128)S(1)}, f32[2,4,8,320]{3,2,1,0:T(8,128)S(1)}, u32[]{:S(2)}, u32[]{:S(2)}) collective-permute-start(f32[2,4,8,320]{3,2,1,0:T(8,128)S(1)} %get-tuple-element.250), channel_id=1, source_target_pairs={{0,4},{4,8},{8,12},{1,5},{5,9},{9,13},{2,6},{6,10},{10,14},{3,7},{... | collective-permute-start | bytes 245768 | tf_op jit(solution)/shard_map/ppermute | solution.py:14
  9.7 9.4 %all-reduce.20 = s32[1024]{0:T(1024)S(1)} all-reduce(s32[1024]{0:T(1024)S(1)} %bitcast_dynamic-update-slice_fusion), channel_id=1, replica_groups=mesh['shot'=2,'gx'=4,'gy'=4] {'gx','gy'}, use_global_device_ids=true, to_apply=%add.20 | all-reduce | flops 1024 | bytes 8192
  19.3 1.9 collective-permute-start.3
  21.3 2.4 collective-permute-start.2
  23.8 15.2 %all-gather = f32[16,64,10]{1,2,0:T(8,128)S(1)} all-gather(f32[1,64,10]{1,2,0:T(8,128)S(1)} %bitcast.208), channel_id=1, replica_groups=mesh['shot'=2,'gx'=4,'gy'=4] {'gx','gy'}, dimensions={0}, use_global_device_ids=true | all-gather | bytes 43520 | tf_op jit(solution)/shard_map/all_gather | solution.py:68
  39.2 6.0 %scatter_custom_fusion = f32[10,64]{0,1:T(8,128)S(1)} fusion(s32[1024]{0:T(1024)S(1)} %bitcast.209, f32[1024,10]{1,0:T(8,128)S(1)} %bitcast.206, f32[]{:T(128)} %constant.323.clone.1), kind=kCustom, calls=%fused_computation.926 | custom fusion | flops 10240 | bytes 2564 | tf_op jit(solution)/shard_map/scatter-add | solution.py:78
  49.3 3.3 %collective-permute-start.5 = (f32[2,4,8,320]{3,2,1,0:T(8,128)S(1)}, f32[2,4,8,320]{3,2,1,0:T(8,128)S(1)}, u32[]{:S(2)}, u32[]{:S(2)}) collective-permute-start(f32[2,4,8,320]{3,2,1,0:T(8,128)S(1)} %get-tuple-element.249), channel_id=1, source_target_pairs={{4,0},{8,4},{12,8},{5,1},{9,5},{13,9},{6,2},{10,6},{14,10},{7,3},{... | collective-permute-start | bytes 245768 | tf_op jit(solution)/shard_map/ppermute | solution.py:17
  52.6 2.6 %collective-permute-start.4 = (f32[2,4,8,320]{3,2,1,0:T(8,128)S(1)}, f32[2,4,8,320]{3,2,1,0:T(8,128)S(1)}, u32[]{:S(2)}, u32[]{:S(2)}) collective-permute-start(f32[2,4,8,320]{3,2,1,0:T(8,128)S(1)} %get-tuple-element.248), channel_id=1, source_target_pairs={{0,4},{4,8},{8,12},{1,5},{5,9},{9,13},{2,6},{6,10},{10,14},{3,7},{... | collective-permute-start | bytes 245768 | tf_op jit(solution)/shard_map/ppermute | solution.py:14
  56.3 4.3 %collective-permute-done.4 = f32[2,4,8,320]{3,2,1,0:T(8,128)S(1)} collective-permute-done((f32[2,4,8,320]{3,2,1,0:T(8,128)S(1)}, f32[2,4,8,320]{3,2,1,0:T(8,128)S(1)}, u32[]{:S(2)}, u32[]{:S(2)}) %collective-permute-start.4) | collective-permute-done | bytes 81952 | tf_op jit(solution)/shard_map/ppermute | solution.py:14
  60.7 3.6 %collective-permute-start.7 = (f32[2,16,4,320]{3,1,2,0:T(8,128)S(1)}, f32[2,16,4,320]{3,1,2,0:T(8,128)S(1)}, u32[]{:S(2)}, u32[]{:S(2)}) collective-permute-start(f32[2,16,4,320]{3,1,2,0:T(8,128)S(1)} %copy.731), channel_id=1, source_target_pairs={{1,0},{2,1},{3,2},{5,4},{6,5},{7,6},{9,8},{10,9},{11,10},{13,12},{... | collective-permute-start | bytes 491528 | tf_op jit(solution)/shard_map/ppermute | solution.py:17
  64.4 1.9 collective-permute-start.6
  67.6 3.8 %collective-permute-done.6 = f32[2,16,4,320]{3,1,2,0:T(8,128)S(1)} collective-permute-done((f32[2,16,4,320]{3,1,2,0:T(8,128)S(1)}, f32[2,16,4,320]{3,1,2,0:T(8,128)S(1)}, u32[]{:S(2)}, u32[]{:S(2)}) %collective-permute-start.6) | collective-permute-done | bytes 163872 | tf_op jit(solution)/shard_map/ppermute | solution.py:14
  73.1 3.4 %collective-permute-start.9 = (f32[2,4,8,320]{3,2,1,0:T(8,128)S(1)}, f32[2,4,8,320]{3,2,1,0:T(8,128)S(1)}, u32[]{:S(2)}, u32[]{:S(2)}) collective-permute-start(f32[2,4,8,320]{3,2,1,0:T(8,128)S(1)} %get-tuple-element.247), channel_id=1, source_target_pairs={{4,0},{8,4},{12,8},{5,1},{9,5},{13,9},{6,2},{10,6},{14,10},{7,3},{... | collective-permute-start | bytes 245768 | tf_op jit(solution)/shard_map/ppermute | solution.py:17
  76.4 2.5 collective-permute-start.8
  79.6 3.4 %collective-permute-done.8 = f32[2,4,8,320]{3,2,1,0:T(8,128)S(1)} collective-permute-done((f32[2,4,8,320]{3,2,1,0:T(8,128)S(1)}, f32[2,4,8,320]{3,2,1,0:T(8,128)S(1)}, u32[]{:S(2)}, u32[]{:S(2)}) %collective-permute-start.8) | collective-permute-done | bytes 81952 | tf_op jit(solution)/shard_map/ppermute | solution.py:14
  83.1 1.9 collective-permute-start.11
  85.0 2.4 collective-permute-start.10
  88.2 3.8 %collective-permute-done.10 = f32[2,16,4,320]{3,1,2,0:T(8,128)S(1)} collective-permute-done((f32[2,16,4,320]{3,1,2,0:T(8,128)S(1)}, f32[2,16,4,320]{3,1,2,0:T(8,128)S(1)}, u32[]{:S(2)}, u32[]{:S(2)}) %collective-permute-start.10) | collective-permute-done | bytes 163872 | tf_op jit(solution)/shard_map/ppermute | solution.py:14
  95.7 3.9 %collective-permute-start.12 = (f32[2,4,8,320]{3,2,1,0:T(8,128)S(1)}, f32[2,4,8,320]{3,2,1,0:T(8,128)S(1)}, u32[]{:S(2)}, u32[]{:S(2)}) collective-permute-start(f32[2,4,8,320]{3,2,1,0:T(8,128)S(1)} %get-tuple-element.244), channel_id=1, source_target_pairs={{0,4},{4,8},{8,12},{1,5},{5,9},{9,13},{2,6},{6,10},{10,14},{3,7},{... | collective-permute-start | bytes 245768 | tf_op jit(solution)/shard_map/ppermute | solution.py:14
  100.2 1.9 collective-permute-done.12
  104.2 2.4 collective-permute-start.14
  107.5 3.8 %collective-permute-done.14 = f32[2,16,4,320]{3,1,2,0:T(8,128)S(1)} collective-permute-done((f32[2,16,4,320]{3,1,2,0:T(8,128)S(1)}, f32[2,16,4,320]{3,1,2,0:T(8,128)S(1)}, u32[]{:S(2)}, u32[]{:S(2)}) %collective-permute-start.14) | collective-permute-done | bytes 163872 | tf_op jit(solution)/shard_map/ppermute | solution.py:14
  114.9 3.9 %collective-permute-start.16 = (f32[2,4,8,320]{3,2,1,0:T(8,128)S(1)}, f32[2,4,8,320]{3,2,1,0:T(8,128)S(1)}, u32[]{:S(2)}, u32[]{:S(2)}) collective-permute-start(f32[2,4,8,320]{3,2,1,0:T(8,128)S(1)} %get-tuple-element.242), channel_id=1, source_target_pairs={{0,4},{4,8},{8,12},{1,5},{5,9},{9,13},{2,6},{6,10},{10,14},{3,7},{... | collective-permute-start | bytes 245768 | tf_op jit(solution)/shard_map/ppermute | solution.py:14
  119.5 1.9 collective-permute-done.16
  123.5 2.4 collective-permute-start.18
  126.7 3.8 %collective-permute-done.18 = f32[2,16,4,320]{3,1,2,0:T(8,128)S(1)} collective-permute-done((f32[2,16,4,320]{3,1,2,0:T(8,128)S(1)}, f32[2,16,4,320]{3,1,2,0:T(8,128)S(1)}, u32[]{:S(2)}, u32[]{:S(2)}) %collective-permute-start.18) | collective-permute-done | bytes 163872 | tf_op jit(solution)/shard_map/ppermute | solution.py:14
  134.2 3.9 %collective-permute-start.20 = (f32[2,4,8,320]{3,2,1,0:T(8,128)S(1)}, f32[2,4,8,320]{3,2,1,0:T(8,128)S(1)}, u32[]{:S(2)}, u32[]{:S(2)}) collective-permute-start(f32[2,4,8,320]{3,2,1,0:T(8,128)S(1)} %get-tuple-element.240), channel_id=1, source_target_pairs={{0,4},{4,8},{8,12},{1,5},{5,9},{9,13},{2,6},{6,10},{10,14},{3,7},{... | collective-permute-start | bytes 245768 | tf_op jit(solution)/shard_map/ppermute | solution.py:14
  138.7 1.9 collective-permute-done.20
  142.7 2.6 %collective-permute-start.22 = (f32[2,16,4,320]{3,1,2,0:T(8,128)S(1)}, f32[2,16,4,320]{3,1,2,0:T(8,128)S(1)}, u32[]{:S(2)}, u32[]{:S(2)}) collective-permute-start(f32[2,16,4,320]{3,1,2,0:T(8,128)S(1)} %copy.738), channel_id=1, source_target_pairs={{0,1},{1,2},{2,3},{4,5},{5,6},{6,7},{8,9},{9,10},{10,11},{12,13},{... | collective-permute-start | bytes 491528 | tf_op jit(solution)/shard_map/ppermute | solution.py:14
  146.0 3.8 %collective-permute-done.22 = f32[2,16,4,320]{3,1,2,0:T(8,128)S(1)} collective-permute-done((f32[2,16,4,320]{3,1,2,0:T(8,128)S(1)}, f32[2,16,4,320]{3,1,2,0:T(8,128)S(1)}, u32[]{:S(2)}, u32[]{:S(2)}) %collective-permute-start.22) | collective-permute-done | bytes 163872 | tf_op jit(solution)/shard_map/ppermute | solution.py:14
  153.4 3.9 %collective-permute-start.24 = (f32[2,4,8,320]{3,2,1,0:T(8,128)S(1)}, f32[2,4,8,320]{3,2,1,0:T(8,128)S(1)}, u32[]{:S(2)}, u32[]{:S(2)}) collective-permute-start(f32[2,4,8,320]{3,2,1,0:T(8,128)S(1)} %get-tuple-element.238), channel_id=1, source_target_pairs={{0,4},{4,8},{8,12},{1,5},{5,9},{9,13},{2,6},{6,10},{10,14},{3,7},{... | collective-permute-start | bytes 245768 | tf_op jit(solution)/shard_map/ppermute | solution.py:14
  158.0 1.9 collective-permute-done.24
  162.0 2.4 collective-permute-start.26
  165.2 3.8 %collective-permute-done.26 = f32[2,16,4,320]{3,1,2,0:T(8,128)S(1)} collective-permute-done((f32[2,16,4,320]{3,1,2,0:T(8,128)S(1)}, f32[2,16,4,320]{3,1,2,0:T(8,128)S(1)}, u32[]{:S(2)}, u32[]{:S(2)}) %collective-permute-start.26) | collective-permute-done | bytes 163872 | tf_op jit(solution)/shard_map/ppermute | solution.py:14
  172.7 3.9 %collective-permute-start.28 = (f32[2,4,8,320]{3,2,1,0:T(8,128)S(1)}, f32[2,4,8,320]{3,2,1,0:T(8,128)S(1)}, u32[]{:S(2)}, u32[]{:S(2)}) collective-permute-start(f32[2,4,8,320]{3,2,1,0:T(8,128)S(1)} %get-tuple-element.236), channel_id=1, source_target_pairs={{0,4},{4,8},{8,12},{1,5},{5,9},{9,13},{2,6},{6,10},{10,14},{3,7},{... | collective-permute-start | bytes 245768 | tf_op jit(solution)/shard_map/ppermute | solution.py:14
  177.3 1.9 collective-permute-done.28
  181.3 2.4 collective-permute-start.30
  184.5 3.8 %collective-permute-done.30 = f32[2,16,4,320]{3,1,2,0:T(8,128)S(1)} collective-permute-done((f32[2,16,4,320]{3,1,2,0:T(8,128)S(1)}, f32[2,16,4,320]{3,1,2,0:T(8,128)S(1)}, u32[]{:S(2)}, u32[]{:S(2)}) %collective-permute-start.30) | collective-permute-done | bytes 163872 | tf_op jit(solution)/shard_map/ppermute | solution.py:14
  191.9 3.9 %collective-permute-start.32 = (f32[2,4,8,320]{3,2,1,0:T(8,128)S(1)}, f32[2,4,8,320]{3,2,1,0:T(8,128)S(1)}, u32[]{:S(2)}, u32[]{:S(2)}) collective-permute-start(f32[2,4,8,320]{3,2,1,0:T(8,128)S(1)} %get-tuple-element.234), channel_id=1, source_target_pairs={{0,4},{4,8},{8,12},{1,5},{5,9},{9,13},{2,6},{6,10},{10,14},{3,7},{... | collective-permute-start | bytes 245768 | tf_op jit(solution)/shard_map/ppermute | solution.py:14
  196.5 1.9 collective-permute-done.32
  200.5 2.4 collective-permute-start.34
  203.8 3.8 %collective-permute-done.34 = f32[2,16,4,320]{3,1,2,0:T(8,128)S(1)} collective-permute-done((f32[2,16,4,320]{3,1,2,0:T(8,128)S(1)}, f32[2,16,4,320]{3,1,2,0:T(8,128)S(1)}, u32[]{:S(2)}, u32[]{:S(2)}) %collective-permute-start.34) | collective-permute-done | bytes 163872 | tf_op jit(solution)/shard_map/ppermute | solution.py:14
  209.3 2.1 collective-permute-start.37
  211.4 3.9 %collective-permute-start.36 = (f32[2,4,8,320]{3,2,1,0:T(8,128)S(1)}, f32[2,4,8,320]{3,2,1,0:T(8,128)S(1)}, u32[]{:S(2)}, u32[]{:S(2)}) collective-permute-start(f32[2,4,8,320]{3,2,1,0:T(8,128)S(1)} %get-tuple-element.232), channel_id=1, source_target_pairs={{0,4},{4,8},{8,12},{1,5},{5,9},{9,13},{2,6},{6,10},{10,14},{3,7},{... | collective-permute-start | bytes 245768 | tf_op jit(solution)/shard_map/ppermute | solution.py:14
  237.1 2.4 collective-permute-start.38
  240.4 3.7 %collective-permute-done.38 = f32[2,16,4,320]{3,1,2,0:T(8,128)S(1)} collective-permute-done((f32[2,16,4,320]{3,1,2,0:T(8,128)S(1)}, f32[2,16,4,320]{3,1,2,0:T(8,128)S(1)}, u32[]{:S(2)}, u32[]{:S(2)}) %collective-permute-start.38) | collective-permute-done | bytes 163872 | tf_op jit(solution)/shard_map/ppermute | solution.py:14
  247.3 7.1 %fusion.361 = (f32[8,8,320]{2,1,0:T(8,128)}, f32[8,8,320]{2,1,0:T(8,128)}) fusion(f32[8,8,320]{2,1,0:T(8,128)S(1)} %multiply_add_fusion.1, f32[8,8,320]{2,1,0:T(8,128)S(1)} %multiply_add_fusion.3, f32[8,8,320]{2,1,0:T(8,128)S(1)} %multiply_add_fusion.4, f32[8,8,320]{2,1,0:T(8,128)S(1)} %multiply_add_fusion.8, f32[8,8,320]{2,1,0:T(8,128)S(1)} %copy-done.7, ...), kind=kLoop, calls=%fused_computation.864 | loop fusion | flops 1228800 | bytes 1556530 | tf_op jit(solution)/shard_map/add | solution.py:116
  (215 shorter events, 63.0 us)
Async XLA Ops:
  0.6 7.7 %copy-start.13 = (u32[32]{0:T(128)S(1)}, u32[32]{0:T(128)}, u32[]{:S(2)}) copy-start(u32[32]{0:T(128)} %constant.395) | copy-start | bytes 388
  0.6 8.9 %copy-start.12 = (s32[1,64]{1,0:T(1,128)S(1)}, s32[1,64]{1,0:T(1,128)}, u32[]{:S(2)}) copy-start(s32[1,64]{1,0:T(1,128)} %param.40) | copy-start | bytes 772
  0.7 18.6 %copy-start.4 = (f32[8,8,320]{2,1,0:T(8,128)S(1)}, f32[8,8,320]{2,1,0:T(8,128)}, u32[]{:S(2)}) copy-start(f32[8,8,320]{2,1,0:T(8,128)} %param.35) | copy-start | bytes 245764
  1.6 17.6 %copy-start.1 = (f32[8,8,320]{2,1,0:T(8,128)S(1)}, f32[8,8,320]{2,1,0:T(8,128)}, u32[]{:S(2)}) copy-start(f32[8,8,320]{2,1,0:T(8,128)} %param.33) | copy-start | bytes 245764
  1.6 17.6 %collective-permute-start.1 = (f32[2,4,8,320]{3,2,1,0:T(8,128)S(1)}, f32[2,4,8,320]{3,2,1,0:T(8,128)S(1)}, u32[]{:S(2)}, u32[]{:S(2)}) collective-permute-start(f32[2,4,8,320]{3,2,1,0:T(8,128)S(1)} %get-tuple-element.251), channel_id=1, source_target_pairs={{4,0},{8,4},{12,8},{5,1},{9,5},{13,9},{6,2},{10,6},{14,10},{7,3},{... | collective-permute-start | bytes 245768 | tf_op jit(solution)/shard_map/ppermute | solution.py:17
  4.1 15.1 %collective-permute-start = (f32[2,4,8,320]{3,2,1,0:T(8,128)S(1)}, f32[2,4,8,320]{3,2,1,0:T(8,128)S(1)}, u32[]{:S(2)}, u32[]{:S(2)}) collective-permute-start(f32[2,4,8,320]{3,2,1,0:T(8,128)S(1)} %get-tuple-element.250), channel_id=1, source_target_pairs={{0,4},{4,8},{8,12},{1,5},{5,9},{9,13},{2,6},{6,10},{10,14},{3,7},{... | collective-permute-start | bytes 245768 | tf_op jit(solution)/shard_map/ppermute | solution.py:14
  19.3 26.6 %collective-permute-start.3 = (f32[2,16,4,320]{3,1,2,0:T(8,128)S(1)}, f32[2,16,4,320]{3,1,2,0:T(8,128)S(1)}, u32[]{:S(2)}, u32[]{:S(2)}) collective-permute-start(f32[2,16,4,320]{3,1,2,0:T(8,128)S(1)} %copy.729), channel_id=1, source_target_pairs={{1,0},{2,1},{3,2},{5,4},{6,5},{7,6},{9,8},{10,9},{11,10},{13,12},{... | collective-permute-start | bytes 491528 | tf_op jit(solution)/shard_map/ppermute | solution.py:17
  21.3 24.7 %collective-permute-start.2 = (f32[2,16,4,320]{3,1,2,0:T(8,128)S(1)}, f32[2,16,4,320]{3,1,2,0:T(8,128)S(1)}, u32[]{:S(2)}, u32[]{:S(2)}) collective-permute-start(f32[2,16,4,320]{3,1,2,0:T(8,128)S(1)} %copy.728), channel_id=1, source_target_pairs={{0,1},{1,2},{2,3},{4,5},{5,6},{6,7},{8,9},{9,10},{10,11},{12,13},{... | collective-permute-start | bytes 491528 | tf_op jit(solution)/shard_map/ppermute | solution.py:14
  39.0 6.3 %copy-start.9 = (f32[10]{0:T(128)S(1)}, f32[10]{0:T(128)}, u32[]{:S(2)}) copy-start(f32[10]{0:T(128)} %param.37) | copy-start | bytes 124
  49.3 6.9 %collective-permute-start.5 = (f32[2,4,8,320]{3,2,1,0:T(8,128)S(1)}, f32[2,4,8,320]{3,2,1,0:T(8,128)S(1)}, u32[]{:S(2)}, u32[]{:S(2)}) collective-permute-start(f32[2,4,8,320]{3,2,1,0:T(8,128)S(1)} %get-tuple-element.249), channel_id=1, source_target_pairs={{4,0},{8,4},{12,8},{5,1},{9,5},{13,9},{6,2},{10,6},{14,10},{7,3},{... | collective-permute-start | bytes 245768 | tf_op jit(solution)/shard_map/ppermute | solution.py:17
  52.6 8.0 %collective-permute-start.4 = (f32[2,4,8,320]{3,2,1,0:T(8,128)S(1)}, f32[2,4,8,320]{3,2,1,0:T(8,128)S(1)}, u32[]{:S(2)}, u32[]{:S(2)}) collective-permute-start(f32[2,4,8,320]{3,2,1,0:T(8,128)S(1)} %get-tuple-element.248), channel_id=1, source_target_pairs={{0,4},{4,8},{8,12},{1,5},{5,9},{9,13},{2,6},{6,10},{10,14},{3,7},{... | collective-permute-start | bytes 245768 | tf_op jit(solution)/shard_map/ppermute | solution.py:14
  60.7 6.8 %collective-permute-start.7 = (f32[2,16,4,320]{3,1,2,0:T(8,128)S(1)}, f32[2,16,4,320]{3,1,2,0:T(8,128)S(1)}, u32[]{:S(2)}, u32[]{:S(2)}) collective-permute-start(f32[2,16,4,320]{3,1,2,0:T(8,128)S(1)} %copy.731), channel_id=1, source_target_pairs={{1,0},{2,1},{3,2},{5,4},{6,5},{7,6},{9,8},{10,9},{11,10},{13,12},{... | collective-permute-start | bytes 491528 | tf_op jit(solution)/shard_map/ppermute | solution.py:17
  64.4 7.0 %collective-permute-start.6 = (f32[2,16,4,320]{3,1,2,0:T(8,128)S(1)}, f32[2,16,4,320]{3,1,2,0:T(8,128)S(1)}, u32[]{:S(2)}, u32[]{:S(2)}) collective-permute-start(f32[2,16,4,320]{3,1,2,0:T(8,128)S(1)} %copy.730), channel_id=1, source_target_pairs={{0,1},{1,2},{2,3},{4,5},{5,6},{6,7},{8,9},{9,10},{10,11},{12,13},{... | collective-permute-start | bytes 491528 | tf_op jit(solution)/shard_map/ppermute | solution.py:14
  73.1 6.5 %collective-permute-start.9 = (f32[2,4,8,320]{3,2,1,0:T(8,128)S(1)}, f32[2,4,8,320]{3,2,1,0:T(8,128)S(1)}, u32[]{:S(2)}, u32[]{:S(2)}) collective-permute-start(f32[2,4,8,320]{3,2,1,0:T(8,128)S(1)} %get-tuple-element.247), channel_id=1, source_target_pairs={{4,0},{8,4},{12,8},{5,1},{9,5},{13,9},{6,2},{10,6},{14,10},{7,3},{... | collective-permute-start | bytes 245768 | tf_op jit(solution)/shard_map/ppermute | solution.py:17
  76.4 6.5 %collective-permute-start.8 = (f32[2,4,8,320]{3,2,1,0:T(8,128)S(1)}, f32[2,4,8,320]{3,2,1,0:T(8,128)S(1)}, u32[]{:S(2)}, u32[]{:S(2)}) collective-permute-start(f32[2,4,8,320]{3,2,1,0:T(8,128)S(1)} %get-tuple-element.246), channel_id=1, source_target_pairs={{0,4},{4,8},{8,12},{1,5},{5,9},{9,13},{2,6},{6,10},{10,14},{3,7},{... | collective-permute-start | bytes 245768 | tf_op jit(solution)/shard_map/ppermute | solution.py:14
  83.1 5.1 %collective-permute-start.11 = (f32[2,16,4,320]{3,1,2,0:T(8,128)S(1)}, f32[2,16,4,320]{3,1,2,0:T(8,128)S(1)}, u32[]{:S(2)}, u32[]{:S(2)}) collective-permute-start(f32[2,16,4,320]{3,1,2,0:T(8,128)S(1)} %copy.733), channel_id=1, source_target_pairs={{1,0},{2,1},{3,2},{5,4},{6,5},{7,6},{9,8},{10,9},{11,10},{13,12},{... | collective-permute-start | bytes 491528 | tf_op jit(solution)/shard_map/ppermute | solution.py:17
  85.0 7.0 %collective-permute-start.10 = (f32[2,16,4,320]{3,1,2,0:T(8,128)S(1)}, f32[2,16,4,320]{3,1,2,0:T(8,128)S(1)}, u32[]{:S(2)}, u32[]{:S(2)}) collective-permute-start(f32[2,16,4,320]{3,1,2,0:T(8,128)S(1)} %copy.732), channel_id=1, source_target_pairs={{0,1},{1,2},{2,3},{4,5},{5,6},{6,7},{8,9},{9,10},{10,11},{12,13},{... | collective-permute-start | bytes 491528 | tf_op jit(solution)/shard_map/ppermute | solution.py:14
  93.7 6.5 %collective-permute-start.13 = (f32[2,4,8,320]{3,2,1,0:T(8,128)S(1)}, f32[2,4,8,320]{3,2,1,0:T(8,128)S(1)}, u32[]{:S(2)}, u32[]{:S(2)}) collective-permute-start(f32[2,4,8,320]{3,2,1,0:T(8,128)S(1)} %get-tuple-element.245), channel_id=1, source_target_pairs={{4,0},{8,4},{12,8},{5,1},{9,5},{13,9},{6,2},{10,6},{14,10},{7,3},{... | collective-permute-start | bytes 245768 | tf_op jit(solution)/shard_map/ppermute | solution.py:17
  95.7 6.5 %collective-permute-start.12 = (f32[2,4,8,320]{3,2,1,0:T(8,128)S(1)}, f32[2,4,8,320]{3,2,1,0:T(8,128)S(1)}, u32[]{:S(2)}, u32[]{:S(2)}) collective-permute-start(f32[2,4,8,320]{3,2,1,0:T(8,128)S(1)} %get-tuple-element.244), channel_id=1, source_target_pairs={{0,4},{4,8},{8,12},{1,5},{5,9},{9,13},{2,6},{6,10},{10,14},{3,7},{... | collective-permute-start | bytes 245768 | tf_op jit(solution)/shard_map/ppermute | solution.py:14
  102.3 5.1 %collective-permute-start.15 = (f32[2,16,4,320]{3,1,2,0:T(8,128)S(1)}, f32[2,16,4,320]{3,1,2,0:T(8,128)S(1)}, u32[]{:S(2)}, u32[]{:S(2)}) collective-permute-start(f32[2,16,4,320]{3,1,2,0:T(8,128)S(1)} %copy.735), channel_id=1, source_target_pairs={{1,0},{2,1},{3,2},{5,4},{6,5},{7,6},{9,8},{10,9},{11,10},{13,12},{... | collective-permute-start | bytes 491528 | tf_op jit(solution)/shard_map/ppermute | solution.py:17
  104.2 7.0 %collective-permute-start.14 = (f32[2,16,4,320]{3,1,2,0:T(8,128)S(1)}, f32[2,16,4,320]{3,1,2,0:T(8,128)S(1)}, u32[]{:S(2)}, u32[]{:S(2)}) collective-permute-start(f32[2,16,4,320]{3,1,2,0:T(8,128)S(1)} %copy.734), channel_id=1, source_target_pairs={{0,1},{1,2},{2,3},{4,5},{5,6},{6,7},{8,9},{9,10},{10,11},{12,13},{... | collective-permute-start | bytes 491528 | tf_op jit(solution)/shard_map/ppermute | solution.py:14
  113.0 6.5 %collective-permute-start.17 = (f32[2,4,8,320]{3,2,1,0:T(8,128)S(1)}, f32[2,4,8,320]{3,2,1,0:T(8,128)S(1)}, u32[]{:S(2)}, u32[]{:S(2)}) collective-permute-start(f32[2,4,8,320]{3,2,1,0:T(8,128)S(1)} %get-tuple-element.243), channel_id=1, source_target_pairs={{4,0},{8,4},{12,8},{5,1},{9,5},{13,9},{6,2},{10,6},{14,10},{7,3},{... | collective-permute-start | bytes 245768 | tf_op jit(solution)/shard_map/ppermute | solution.py:17
  114.9 6.5 %collective-permute-start.16 = (f32[2,4,8,320]{3,2,1,0:T(8,128)S(1)}, f32[2,4,8,320]{3,2,1,0:T(8,128)S(1)}, u32[]{:S(2)}, u32[]{:S(2)}) collective-permute-start(f32[2,4,8,320]{3,2,1,0:T(8,128)S(1)} %get-tuple-element.242), channel_id=1, source_target_pairs={{0,4},{4,8},{8,12},{1,5},{5,9},{9,13},{2,6},{6,10},{10,14},{3,7},{... | collective-permute-start | bytes 245768 | tf_op jit(solution)/shard_map/ppermute | solution.py:14
  121.5 5.1 %collective-permute-start.19 = (f32[2,16,4,320]{3,1,2,0:T(8,128)S(1)}, f32[2,16,4,320]{3,1,2,0:T(8,128)S(1)}, u32[]{:S(2)}, u32[]{:S(2)}) collective-permute-start(f32[2,16,4,320]{3,1,2,0:T(8,128)S(1)} %copy.737), channel_id=1, source_target_pairs={{1,0},{2,1},{3,2},{5,4},{6,5},{7,6},{9,8},{10,9},{11,10},{13,12},{... | collective-permute-start | bytes 491528 | tf_op jit(solution)/shard_map/ppermute | solution.py:17
  123.5 7.0 %collective-permute-start.18 = (f32[2,16,4,320]{3,1,2,0:T(8,128)S(1)}, f32[2,16,4,320]{3,1,2,0:T(8,128)S(1)}, u32[]{:S(2)}, u32[]{:S(2)}) collective-permute-start(f32[2,16,4,320]{3,1,2,0:T(8,128)S(1)} %copy.736), channel_id=1, source_target_pairs={{0,1},{1,2},{2,3},{4,5},{5,6},{6,7},{8,9},{9,10},{10,11},{12,13},{... | collective-permute-start | bytes 491528 | tf_op jit(solution)/shard_map/ppermute | solution.py:14
  132.2 6.5 %collective-permute-start.21 = (f32[2,4,8,320]{3,2,1,0:T(8,128)S(1)}, f32[2,4,8,320]{3,2,1,0:T(8,128)S(1)}, u32[]{:S(2)}, u32[]{:S(2)}) collective-permute-start(f32[2,4,8,320]{3,2,1,0:T(8,128)S(1)} %get-tuple-element.241), channel_id=1, source_target_pairs={{4,0},{8,4},{12,8},{5,1},{9,5},{13,9},{6,2},{10,6},{14,10},{7,3},{... | collective-permute-start | bytes 245768 | tf_op jit(solution)/shard_map/ppermute | solution.py:17
  134.2 6.5 %collective-permute-start.20 = (f32[2,4,8,320]{3,2,1,0:T(8,128)S(1)}, f32[2,4,8,320]{3,2,1,0:T(8,128)S(1)}, u32[]{:S(2)}, u32[]{:S(2)}) collective-permute-start(f32[2,4,8,320]{3,2,1,0:T(8,128)S(1)} %get-tuple-element.240), channel_id=1, source_target_pairs={{0,4},{4,8},{8,12},{1,5},{5,9},{9,13},{2,6},{6,10},{10,14},{3,7},{... | collective-permute-start | bytes 245768 | tf_op jit(solution)/shard_map/ppermute | solution.py:14
  140.8 5.1 %collective-permute-start.23 = (f32[2,16,4,320]{3,1,2,0:T(8,128)S(1)}, f32[2,16,4,320]{3,1,2,0:T(8,128)S(1)}, u32[]{:S(2)}, u32[]{:S(2)}) collective-permute-start(f32[2,16,4,320]{3,1,2,0:T(8,128)S(1)} %copy.739), channel_id=1, source_target_pairs={{1,0},{2,1},{3,2},{5,4},{6,5},{7,6},{9,8},{10,9},{11,10},{13,12},{... | collective-permute-start | bytes 491528 | tf_op jit(solution)/shard_map/ppermute | solution.py:17
  142.7 7.0 %collective-permute-start.22 = (f32[2,16,4,320]{3,1,2,0:T(8,128)S(1)}, f32[2,16,4,320]{3,1,2,0:T(8,128)S(1)}, u32[]{:S(2)}, u32[]{:S(2)}) collective-permute-start(f32[2,16,4,320]{3,1,2,0:T(8,128)S(1)} %copy.738), channel_id=1, source_target_pairs={{0,1},{1,2},{2,3},{4,5},{5,6},{6,7},{8,9},{9,10},{10,11},{12,13},{... | collective-permute-start | bytes 491528 | tf_op jit(solution)/shard_map/ppermute | solution.py:14
  151.5 6.5 %collective-permute-start.25 = (f32[2,4,8,320]{3,2,1,0:T(8,128)S(1)}, f32[2,4,8,320]{3,2,1,0:T(8,128)S(1)}, u32[]{:S(2)}, u32[]{:S(2)}) collective-permute-start(f32[2,4,8,320]{3,2,1,0:T(8,128)S(1)} %get-tuple-element.239), channel_id=1, source_target_pairs={{4,0},{8,4},{12,8},{5,1},{9,5},{13,9},{6,2},{10,6},{14,10},{7,3},{... | collective-permute-start | bytes 245768 | tf_op jit(solution)/shard_map/ppermute | solution.py:17
  153.4 6.5 %collective-permute-start.24 = (f32[2,4,8,320]{3,2,1,0:T(8,128)S(1)}, f32[2,4,8,320]{3,2,1,0:T(8,128)S(1)}, u32[]{:S(2)}, u32[]{:S(2)}) collective-permute-start(f32[2,4,8,320]{3,2,1,0:T(8,128)S(1)} %get-tuple-element.238), channel_id=1, source_target_pairs={{0,4},{4,8},{8,12},{1,5},{5,9},{9,13},{2,6},{6,10},{10,14},{3,7},{... | collective-permute-start | bytes 245768 | tf_op jit(solution)/shard_map/ppermute | solution.py:14
  160.1 5.1 %collective-permute-start.27 = (f32[2,16,4,320]{3,1,2,0:T(8,128)S(1)}, f32[2,16,4,320]{3,1,2,0:T(8,128)S(1)}, u32[]{:S(2)}, u32[]{:S(2)}) collective-permute-start(f32[2,16,4,320]{3,1,2,0:T(8,128)S(1)} %copy.741), channel_id=1, source_target_pairs={{1,0},{2,1},{3,2},{5,4},{6,5},{7,6},{9,8},{10,9},{11,10},{13,12},{... | collective-permute-start | bytes 491528 | tf_op jit(solution)/shard_map/ppermute | solution.py:17
  162.0 7.0 %collective-permute-start.26 = (f32[2,16,4,320]{3,1,2,0:T(8,128)S(1)}, f32[2,16,4,320]{3,1,2,0:T(8,128)S(1)}, u32[]{:S(2)}, u32[]{:S(2)}) collective-permute-start(f32[2,16,4,320]{3,1,2,0:T(8,128)S(1)} %copy.740), channel_id=1, source_target_pairs={{0,1},{1,2},{2,3},{4,5},{5,6},{6,7},{8,9},{9,10},{10,11},{12,13},{... | collective-permute-start | bytes 491528 | tf_op jit(solution)/shard_map/ppermute | solution.py:14
  170.8 6.5 %collective-permute-start.29 = (f32[2,4,8,320]{3,2,1,0:T(8,128)S(1)}, f32[2,4,8,320]{3,2,1,0:T(8,128)S(1)}, u32[]{:S(2)}, u32[]{:S(2)}) collective-permute-start(f32[2,4,8,320]{3,2,1,0:T(8,128)S(1)} %get-tuple-element.237), channel_id=1, source_target_pairs={{4,0},{8,4},{12,8},{5,1},{9,5},{13,9},{6,2},{10,6},{14,10},{7,3},{... | collective-permute-start | bytes 245768 | tf_op jit(solution)/shard_map/ppermute | solution.py:17
  172.7 6.5 %collective-permute-start.28 = (f32[2,4,8,320]{3,2,1,0:T(8,128)S(1)}, f32[2,4,8,320]{3,2,1,0:T(8,128)S(1)}, u32[]{:S(2)}, u32[]{:S(2)}) collective-permute-start(f32[2,4,8,320]{3,2,1,0:T(8,128)S(1)} %get-tuple-element.236), channel_id=1, source_target_pairs={{0,4},{4,8},{8,12},{1,5},{5,9},{9,13},{2,6},{6,10},{10,14},{3,7},{... | collective-permute-start | bytes 245768 | tf_op jit(solution)/shard_map/ppermute | solution.py:14
  179.3 5.1 %collective-permute-start.31 = (f32[2,16,4,320]{3,1,2,0:T(8,128)S(1)}, f32[2,16,4,320]{3,1,2,0:T(8,128)S(1)}, u32[]{:S(2)}, u32[]{:S(2)}) collective-permute-start(f32[2,16,4,320]{3,1,2,0:T(8,128)S(1)} %copy.743), channel_id=1, source_target_pairs={{1,0},{2,1},{3,2},{5,4},{6,5},{7,6},{9,8},{10,9},{11,10},{13,12},{... | collective-permute-start | bytes 491528 | tf_op jit(solution)/shard_map/ppermute | solution.py:17
  181.3 7.0 %collective-permute-start.30 = (f32[2,16,4,320]{3,1,2,0:T(8,128)S(1)}, f32[2,16,4,320]{3,1,2,0:T(8,128)S(1)}, u32[]{:S(2)}, u32[]{:S(2)}) collective-permute-start(f32[2,16,4,320]{3,1,2,0:T(8,128)S(1)} %copy.742), channel_id=1, source_target_pairs={{0,1},{1,2},{2,3},{4,5},{5,6},{6,7},{8,9},{9,10},{10,11},{12,13},{... | collective-permute-start | bytes 491528 | tf_op jit(solution)/shard_map/ppermute | solution.py:14
  190.0 6.5 %collective-permute-start.33 = (f32[2,4,8,320]{3,2,1,0:T(8,128)S(1)}, f32[2,4,8,320]{3,2,1,0:T(8,128)S(1)}, u32[]{:S(2)}, u32[]{:S(2)}) collective-permute-start(f32[2,4,8,320]{3,2,1,0:T(8,128)S(1)} %get-tuple-element.235), channel_id=1, source_target_pairs={{4,0},{8,4},{12,8},{5,1},{9,5},{13,9},{6,2},{10,6},{14,10},{7,3},{... | collective-permute-start | bytes 245768 | tf_op jit(solution)/shard_map/ppermute | solution.py:17
  191.9 6.5 %collective-permute-start.32 = (f32[2,4,8,320]{3,2,1,0:T(8,128)S(1)}, f32[2,4,8,320]{3,2,1,0:T(8,128)S(1)}, u32[]{:S(2)}, u32[]{:S(2)}) collective-permute-start(f32[2,4,8,320]{3,2,1,0:T(8,128)S(1)} %get-tuple-element.234), channel_id=1, source_target_pairs={{0,4},{4,8},{8,12},{1,5},{5,9},{9,13},{2,6},{6,10},{10,14},{3,7},{... | collective-permute-start | bytes 245768 | tf_op jit(solution)/shard_map/ppermute | solution.py:14
  198.6 5.1 %collective-permute-start.35 = (f32[2,16,4,320]{3,1,2,0:T(8,128)S(1)}, f32[2,16,4,320]{3,1,2,0:T(8,128)S(1)}, u32[]{:S(2)}, u32[]{:S(2)}) collective-permute-start(f32[2,16,4,320]{3,1,2,0:T(8,128)S(1)} %copy.745), channel_id=1, source_target_pairs={{1,0},{2,1},{3,2},{5,4},{6,5},{7,6},{9,8},{10,9},{11,10},{13,12},{... | collective-permute-start | bytes 491528 | tf_op jit(solution)/shard_map/ppermute | solution.py:17
  200.5 7.0 %collective-permute-start.34 = (f32[2,16,4,320]{3,1,2,0:T(8,128)S(1)}, f32[2,16,4,320]{3,1,2,0:T(8,128)S(1)}, u32[]{:S(2)}, u32[]{:S(2)}) collective-permute-start(f32[2,16,4,320]{3,1,2,0:T(8,128)S(1)} %copy.744), channel_id=1, source_target_pairs={{0,1},{1,2},{2,3},{4,5},{5,6},{6,7},{8,9},{9,10},{10,11},{12,13},{... | collective-permute-start | bytes 491528 | tf_op jit(solution)/shard_map/ppermute | solution.py:14
  208.3 38.9 %copy-start.3 = (f32[8,8,320]{2,1,0:T(8,128)}, f32[8,8,320]{2,1,0:T(8,128)S(1)}, u32[]{:S(2)}) copy-start(f32[8,8,320]{2,1,0:T(8,128)S(1)} %multiply_add_fusion.1) | copy-start | bytes 245764
  209.3 35.5 %copy-start.2 = (f32[8,8,320]{2,1,0:T(8,128)}, f32[8,8,320]{2,1,0:T(8,128)S(1)}, u32[]{:S(2)}) copy-start(f32[8,8,320]{2,1,0:T(8,128)S(1)} %get-tuple-element.175) | copy-start | bytes 245764
  209.3 6.0 %copy-start.11 = (s32[4]{0:T(128)S(1)}, s32[4]{0:T(128)}, u32[]{:S(2)}) copy-start(s32[4]{0:T(128)} %param.41) | copy-start | bytes 52
  209.3 25.6 %collective-permute-start.37 = (f32[2,4,8,320]{3,2,1,0:T(8,128)S(1)}, f32[2,4,8,320]{3,2,1,0:T(8,128)S(1)}, u32[]{:S(2)}, u32[]{:S(2)}) collective-permute-start(f32[2,4,8,320]{3,2,1,0:T(8,128)S(1)} %get-tuple-element.233), channel_id=1, source_target_pairs={{4,0},{8,4},{12,8},{5,1},{9,5},{13,9},{6,2},{10,6},{14,10},{7,3},{... | collective-permute-start | bytes 245768 | tf_op jit(solution)/shard_map/ppermute | solution.py:17
  211.4 23.6 %collective-permute-start.36 = (f32[2,4,8,320]{3,2,1,0:T(8,128)S(1)}, f32[2,4,8,320]{3,2,1,0:T(8,128)S(1)}, u32[]{:S(2)}, u32[]{:S(2)}) collective-permute-start(f32[2,4,8,320]{3,2,1,0:T(8,128)S(1)} %get-tuple-element.232), channel_id=1, source_target_pairs={{0,4},{4,8},{8,12},{1,5},{5,9},{9,13},{2,6},{6,10},{10,14},{3,7},{... | collective-permute-start | bytes 245768 | tf_op jit(solution)/shard_map/ppermute | solution.py:14
  235.1 5.2 %collective-permute-start.39 = (f32[2,16,4,320]{3,1,2,0:T(8,128)S(1)}, f32[2,16,4,320]{3,1,2,0:T(8,128)S(1)}, u32[]{:S(2)}, u32[]{:S(2)}) collective-permute-start(f32[2,16,4,320]{3,1,2,0:T(8,128)S(1)} %copy.747), channel_id=1, source_target_pairs={{1,0},{2,1},{3,2},{5,4},{6,5},{7,6},{9,8},{10,9},{11,10},{13,12},{... | collective-permute-start | bytes 491528 | tf_op jit(solution)/shard_map/ppermute | solution.py:17
  237.1 7.0 %collective-permute-start.38 = (f32[2,16,4,320]{3,1,2,0:T(8,128)S(1)}, f32[2,16,4,320]{3,1,2,0:T(8,128)S(1)}, u32[]{:S(2)}, u32[]{:S(2)}) collective-permute-start(f32[2,16,4,320]{3,1,2,0:T(8,128)S(1)} %copy.746), channel_id=1, source_target_pairs={{0,1},{1,2},{2,3},{4,5},{5,6},{6,7},{8,9},{9,10},{10,11},{12,13},{... | collective-permute-start | bytes 491528 | tf_op jit(solution)/shard_map/ppermute | solution.py:14
  (6 other events, 7.1 us)
where the time goes:
time: 256 us; the launch traced here: 254 us
  starting transfers between devices  103 us (40%)
  waiting for transfers between devices  64.8 us (25%)
  other arithmetic  32.2 us (13%)
  blocking collectives  24.6 us (10%)
  between operations  22.2 us (9%)
  local copies, waits for them, and re-layouts  7.13 us (3%)
    ppermute x20, starting transfers between devices, with_halo(): lax.ppermute(lax.slice_in_dim(block, block.shape[dim] - width, None, axis...  59.8 us
    ppermute x20, waiting for transfers between devices, with_halo(): lax.ppermute(lax.slice_in_dim(block, block.shape[dim] - width, None, axis...  53 us
    ppermute x20, starting transfers between devices, with_halo(): lax.ppermute(lax.slice_in_dim(block, 0, width, axis=dim), axis, backward)  43.6 us
    all_gather x1, blocking collectives, body(): values = lax.all_gather(traces, ('gx', 'gy'), axis=1, tiled=True)  15.2 us
    ppermute x20, waiting for transfers between devices, with_halo(): lax.ppermute(lax.slice_in_dim(block, 0, width, axis=dim), axis, backward)  11.7 us
    convert_element_type x10, other arithmetic, body(): source_field.astype(jnp.bfloat16)[None]  9.89 us
    unnamed x1, blocking collectives  9.37 us
    add x1, other arithmetic, body(): imaged = imaged + jnp.where(present, snapshot * receiver_field, 0.0)  7.05 us
  transfers between devices with their start and end apart: 40, of which 33 were waited for; matrix products, arithmetic and copies ran while one was open for 4% of the time, Pallas kernels for 0%

commit v1 on v0

v1 whole, which is shorter than its diff:
```python
import functools
import jax
import jax.numpy as jnp
from jax import lax
from jax.experimental import pallas as pl
from jax.experimental.pallas import tpu as pltpu
from jax.sharding import PartitionSpec as P

STENCIL_COEFFS = (-205.0 / 72.0, 8.0 / 5.0, -1.0 / 5.0, 8.0 / 315.0, -1.0 / 560.0)
LANES = 128
HALF = 4
LOW_X, HIGH_X, LOW_Y, HIGH_Y = range(4)
OPPOSITE = (HIGH_X, LOW_X, HIGH_Y, LOW_Y)
MESH = pl.DeviceIdType.MESH


def kernel(
    total_steps,
    source_prev,
    source_now,
    receiver_prev,
    receiver_now,
    speed_squared,
    wavelet,
    source_cell,
    traces,
    receiver_cells,
    plan,
    stored,
    image_before,
    out_source_prev,
    out_source_now,
    out_receiver_prev,
    out_receiver_now,
    out_snapshots,
    out_image,
    hist,
    speed,
    core,
    sides,
    packed,
    landed,
    records,
    gathered,
    planes,
    inject,
    send_sem,
    recv_sem,
    trace_send,
    trace_recv,
):
    block_x, block_y, depth = source_now.shape
    count_x, count_y = lax.axis_size("gx"), lax.axis_size("gy")
    me_x, me_y = lax.axis_index("gx"), lax.axis_index("gy")
    grid_y = block_y * count_y
    peers = count_x * count_y
    me = me_x * count_y + me_y
    width = speed.shape[2]
    full = depth // LANES
    own = traces.shape[1]
    slots = plan.shape[0]
    exists = (me_x > 0, me_x < count_x - 1, me_y > 0, me_y < count_y - 1)
    there = ({"gx": me_x - 1}, {"gx": me_x + 1}, {"gy": me_y - 1}, {"gy": me_y + 1})

    def peer_of(offset):
        other = lax.rem(me + offset, peers)
        return {"gx": other // count_y, "gy": lax.rem(other, count_y)}

    barrier = pltpu.get_barrier_semaphore()

    def greet(offset, carry):
        pl.semaphore_signal(barrier, inc=1, device_id=peer_of(offset), device_id_type=MESH)
        return carry

    for side in range(4):

        @pl.when(jnp.logical_not(exists[side]))
        def _():
            for field in range(2):
                for parity in range(2):
                    landed[field, parity, side] = jnp.zeros(landed.shape[3:], jnp.float32)

    lax.fori_loop(1, peers, greet, 0)

    row = lax.broadcasted_iota(jnp.int32, (block_y, width), 0)
    lane = lax.broadcasted_iota(jnp.int32, (block_y, width), 1)
    first_half = row < HALF
    tail_lane = lax.broadcasted_iota(jnp.int32, (block_y, LANES), 1)
    in_tail = tail_lane < LANES // 2

    records[...] = jnp.zeros_like(records)
    records[0:total_steps, :] = traces[...]
    records[total_steps : total_steps + 1, :] = receiver_cells[...].astype(jnp.float32)
    for field, (before, now) in enumerate(
        ((source_prev, source_now), (receiver_prev, receiver_now))
    ):
        for index, array in enumerate((before, now)):
            hist[field, index, HALF : HALF + block_x, :, full * LANES :] = jnp.zeros(
                (block_x, block_y, width - full * LANES), jnp.float32
            )
            hist[field, index, HALF : HALF + block_x, :, 0:depth] = array[...]

    def halo_copy(field, parity, side):
        return pltpu.make_async_remote_copy(
            src_ref=packed.at[field, side],
            dst_ref=landed.at[field, parity, OPPOSITE[side]],
            send_sem=send_sem.at[field, side],
            recv_sem=recv_sem.at[field, parity, OPPOSITE[side]],
            device_id=there[side],
            device_id_type=MESH,
        )

    def arrival(field, parity, side):
        return pltpu.make_async_remote_copy(
            src_ref=packed.at[field, side],
            dst_ref=landed.at[field, parity, side],
            send_sem=send_sem.at[field, side],
            recv_sem=recv_sem.at[field, parity, side],
            device_id=there[side],
            device_id_type=MESH,
        )

    def pack(field, side, tiles):
        for i in range(HALF):
            for j in range(full):
                packed[field, side, i * full + j] = tiles[i][:, j * LANES : (j + 1) * LANES]
        tails = [tile[:, full * LANES :] for tile in tiles]
        for i in range(2):
            packed[field, side, HALF * full + i] = tails[i] + pltpu.roll(
                tails[i + 2], LANES // 2, axis=1
            )

    def unpack(field, parity, side):
        tails = []
        for i in range(2):
            both = landed[field, parity, side, HALF * full + i]
            tails.append((both, pltpu.roll(both, LANES // 2, axis=1)))
        result = []
        for i in range(HALF):
            tail = jnp.where(in_tail, tails[i % 2][i // 2], 0.0)
            result.append(
                jnp.concatenate(
                    [landed[field, parity, side, i * full + j] for j in range(full)] + [tail],
                    axis=1,
                )
            )
        return result

    def send(field, index, parity):
        tiles = [hist[field, index, HALF + x] for x in range(block_x)]
        pack(field, LOW_X, tiles[:HALF])
        pack(field, HIGH_X, tiles[block_x - HALF :])
        turned = [pltpu.roll(tiles[i + HALF], HALF, axis=0) for i in range(HALF)]
        pack(field, LOW_Y, [jnp.where(first_half, tiles[i], turned[i]) for i in range(HALF)])
        pack(field, HIGH_Y, [jnp.where(first_half, turned[i], tiles[i]) for i in range(HALF)])
        for side in range(4):

            @pl.when(exists[side])
            def _():
                halo_copy(field, parity, side).start()

    def receive(field, index, parity):
        for side in range(4):

            @pl.when(exists[side])
            def _():
                arrival(field, parity, side).wait()

        low, high = unpack(field, parity, LOW_X), unpack(field, parity, HIGH_X)
        for i in range(HALF):
            hist[field, index, i] = low[i]
            hist[field, index, HALF + block_x + i] = high[i]
        low, high = unpack(field, parity, LOW_Y), unpack(field, parity, HIGH_Y)
        for i in range(HALF):
            sides[field, i] = jnp.where(first_half, high[i], low[i])
            sides[field, i + HALF] = pltpu.roll(
                jnp.where(first_half, low[i], high[i]), HALF, axis=0
            )

    def advance(field, index, extra):
        for x in range(block_x):
            center = hist[field, index, HALF + x]
            side = sides[field, x]
            spread = 3.0 * STENCIL_COEFFS[0] * center
            for k in range(1, HALF + 1):
                around = hist[field, index, HALF + x - k] + hist[field, index, HALF + x + k]
                around += pltpu.roll(center, k, axis=1) + pltpu.roll(center, width - k, axis=1)
                around += pltpu.roll(jnp.where(row < block_y - k, center, side), k, axis=0)
                around += pltpu.roll(jnp.where(row < k, side, center), block_y - k, axis=0)
                spread += STENCIL_COEFFS[k] * around
            latest = 2.0 * center - hist[field, index - 1, HALF + x] + speed[x] * spread
            hist[field, index + 1, HALF + x] = extra(x, latest)

    pl.semaphore_wait(barrier, peers - 1)
    send(0, 1, 0)
    send(1, 1, 0)

    def trace_copy(offset):
        return pltpu.make_async_remote_copy(
            src_ref=records,
            dst_ref=gathered.at[offset - 1],
            send_sem=trace_send,
            recv_sem=trace_recv,
            device_id=peer_of(offset),
            device_id_type=MESH,
        )

    def spread_records(offset, carry):
        trace_copy(offset).start()
        return carry

    lax.fori_loop(1, peers, spread_records, 0)

    speed[:, :, full * LANES :] = jnp.zeros(
        (block_x, block_y, width - full * LANES), jnp.float32
    )
    speed[:, :, 0:depth] = speed_squared[...]
    for x in range(block_x):
        flat = ((me_x * block_x + x) * grid_y + me_y * block_y + row) * depth + lane
        hit = (flat == source_cell[0]) & (lane < depth)
        core[x] = jnp.where(hit, speed[x], 0.0)

    def source_extra(step):
        return lambda x, latest: latest + wavelet[step] * core[x]

    def receiver_extra(step):
        back = total_steps - 1 - step

        def add(x, latest):
            return jnp.concatenate(
                [latest[:, :LANES] + inject[back, x], latest[:, LANES:]], axis=1
            )

        return add

    def collect_planes():
        everything = pltpu.make_async_remote_copy(
            src_ref=gathered.at[pl.ds(0, peers - 1)],
            dst_ref=gathered.at[pl.ds(0, peers - 1)],
            send_sem=trace_send,
            recv_sem=trace_recv,
            device_id=there[0],
            device_id_type=MESH,
        )
        everything.wait()
        gathered[peers - 1] = records[...]
        cells = block_x * block_y
        number = lax.broadcasted_iota(jnp.int32, (cells, own), 0)
        number = (me_x * block_x + number // block_y) * grid_y + me_y * block_y + number % block_y
        number = number.astype(jnp.float32)

        def one(slot):
            block = gathered[slot]
            chosen = (block[total_steps : total_steps + 1, :] == number).astype(jnp.float32)
            return lax.dot_general(
                chosen,
                block,
                (((1,), (1,)), ((), ())),
                precision=lax.Precision.HIGHEST,
                preferred_element_type=jnp.float32,
            )

        group = 16 if peers % 16 == 0 else 1

        def several(index, total):
            for j in range(group):
                total = total + one(index * group + j)
            return total

        total = lax.fori_loop(
            0, peers // group, several, jnp.zeros((cells, records.shape[0]), jnp.float32)
        )
        planes[...] = jnp.zeros_like(planes)
        planes[:, 0 : records.shape[0]] = total
        for x in range(block_x):
            rows = planes[x * block_y : (x + 1) * block_y, :]
            for step in range(total_steps):
                turned = pltpu.roll(rows, (LANES - step) % LANES, axis=1) if step else rows
                inject[step, x] = jnp.where(tail_lane == 0, turned * speed[x, :, :LANES], 0.0)

    def both(step, carry):
        parity = lax.rem(step, 2)
        for field, extra in enumerate((source_extra, receiver_extra)):
            receive(field, step + 1, parity)
            if field == 1:
                pl.when(step == 0)(collect_planes)
            advance(field, step + 1, extra(step))

            @pl.when(step < total_steps - 1)
            def _():
                send(field, step + 2, 1 - parity)

        return carry

    lax.fori_loop(0, total_steps, both, 0)
    inner = slice(HALF, HALF + block_x)
    out_source_prev[...] = hist[0, total_steps, inner, :, 0:depth]
    out_source_now[...] = hist[0, total_steps + 1, inner, :, 0:depth]
    out_receiver_prev[...] = hist[1, total_steps, inner, :, 0:depth]
    out_receiver_now[...] = hist[1, total_steps + 1, inner, :, 0:depth]
    total = image_before[...]
    for slot in range(slots):
        taken = hist[0, plan[slot] + 2]
        out_snapshots[slot] = taken[inner, :, 0:depth].astype(jnp.bfloat16)
        taken = hist[1, total_steps + 1 - plan[slot]]
        total = total + stored[slot].astype(jnp.float32) * taken[inner, :, 0:depth]
    out_image[...] = total


def body(*arrays):
    source_now, wavelet, traces, stored, plan = (arrays[i] for i in (1, 5, 7, 10, 9))
    block_x, block_y, depth = source_now.shape
    total_steps = wavelet.shape[0]
    own = traces.shape[1]
    peers = lax.axis_size("gx") * lax.axis_size("gy")
    width = -(-depth // LANES) * LANES
    record_rows = -(-(total_steps + 1) // 8) * 8
    tiles = HALF * depth // LANES
    vmem = pl.BlockSpec(memory_space=pltpu.VMEM)
    smem = pl.BlockSpec(memory_space=pltpu.SMEM)
    field = jax.ShapeDtypeStruct(source_now.shape, jnp.float32)
    f32 = jnp.float32
    return pl.pallas_call(
        functools.partial(kernel, total_steps),
        out_shape=(
            field,
            field,
            field,
            field,
            jax.ShapeDtypeStruct(stored.shape, jnp.bfloat16),
            field,
        ),
        in_specs=[vmem] * 5 + [smem, smem, vmem, vmem, smem, vmem, vmem],
        out_specs=[vmem] * 6,
        scratch_shapes=[
            pltpu.VMEM((2, total_steps + 2, block_x + 2 * HALF, block_y, width), f32),
            pltpu.VMEM((block_x, block_y, width), f32),
            pltpu.VMEM((block_x, block_y, width), f32),
            pltpu.VMEM((2, block_x, block_y, width), f32),
            pltpu.VMEM((2, 4, tiles, block_y, LANES), f32),
            pltpu.VMEM((2, 2, 4, tiles, block_y, LANES), f32),
            pltpu.VMEM((record_rows, own), f32),
            pltpu.VMEM((peers, record_rows, own), f32),
            pltpu.VMEM((block_x * block_y, LANES), f32),
            pltpu.VMEM((total_steps, block_x, block_y, LANES), f32),
            pltpu.SemaphoreType.DMA((2, 4)),
            pltpu.SemaphoreType.DMA((2, 2, 4)),
            pltpu.SemaphoreType.DMA,
            pltpu.SemaphoreType.DMA,
        ],
        compiler_params=pltpu.CompilerParams(collective_id=0, has_side_effects=True),
    )(*arrays)


def solution(mesh):
    block = P(("shot", "gx"), "gy", None)
    kept = P("shot", "gx", "gy", None)
    return jax.shard_map(
        body,
        mesh=mesh,
        in_specs=(
            block,
            block,
            block,
            block,
            block,
            P("shot"),
            P("shot"),
            P("shot", ("gx", "gy")),
            P("shot", ("gx", "gy")),
            P("shot"),
            kept,
            block,
        ),
        out_specs=(block, block, block, block, kept, block),
        check_vma=False,
    )
```

time: 256 us -> 54.6 us (0.21)
  the two profiles are of different devices: /device:TPU:18 before, /device:TPU:0 now
where the time goes in v1:
time: 54.6 us; the launch traced here: 54.3 us
  Pallas kernels  47.6 us (87%)
  local copies, waits for them, and re-layouts  5.39 us (10%)
  between operations  1.3 us (2%)
    pallas_call x1, Pallas kernels, body(): pl.pallas_call(functools.partial(kernel, total_steps), out_shape=(field,...  47.6 us
    unnamed x16, local copies, waits for them, and re-layouts  5.39 us

profile of v1, /device:TPU:0, one launch (start us, length us, event | category | flops | bytes accessed | tf_op | source)
XLA Modules:
  0.0 54.3 jit_solution(9653999488716790038)
XLA Ops:
  1.3 47.6 %shard_map.163 = (f32[8,8,320]{2,1,0:T(8,128)}, f32[8,8,320]{2,1,0:T(8,128)}, f32[8,8,320]{2,1,0:T(8,128)}, f32[8,8,320]{2,1,0:T(8,128)}, bf16[4,8,8,320]{3,2,1,0:T(8,128)(2,1)}, /*index=5*/f32[8,8,320]{2,1,0:T(8,128)}) custom-call(f32[8,8,320]{2,1,0:T(8,128)} %source_prev.1, f32[8,8,320]{2,1,0:T(8,128)} %source_now.1, f32[8,8,320]{2,1,0:T(8,128)} %receiver_prev.1, ...), custom_call_target="tpu_custom_call" | custom-call | tf_op jit(solution)/shard_map/pallas_call | solution.py:323
  48.9 0.0 copy-start.4
  48.9 1.6 %copy.25 = f32[8,8,320]{2,1,0:T(8,128)} copy(f32[8,8,320]{2,1,0:T(8,128)} %get-tuple-element.12) | data formatting | bytes 163840
  50.5 0.0 copy-done.4
  50.5 0.0 copy-start.3
  50.5 0.0 copy-start.2
  50.5 0.6 %copy.26 = f32[8,8,320]{2,1,0:T(8,128)} copy(f32[8,8,320]{2,1,0:T(8,128)S(1)} %copy-done.4) | data formatting | bytes 163840
  51.2 0.3 copy-done.3
  51.5 0.0 copy-start
  51.5 0.6 %copy.27 = f32[8,8,320]{2,1,0:T(8,128)} copy(f32[8,8,320]{2,1,0:T(8,128)S(1)} %copy-done.3) | data formatting | bytes 163840
  52.1 0.0 copy-done.2
  52.1 0.6 %copy.28 = f32[8,8,320]{2,1,0:T(8,128)} copy(f32[8,8,320]{2,1,0:T(8,128)S(1)} %copy-done.2) | data formatting | bytes 163840
  52.7 0.0 copy-done
  52.7 0.0 copy-start.1
  52.7 0.7 %copy.29 = bf16[4,8,8,320]{3,2,1,0:T(8,128)(2,1)} copy(bf16[4,8,8,320]{3,2,1,0:T(8,128)(2,1)S(1)} %copy-done) | data formatting | bytes 327680
  53.4 0.3 copy-done.1
  53.7 0.6 %copy.30 = f32[8,8,320]{2,1,0:T(8,128)} copy(f32[8,8,320]{2,1,0:T(8,128)S(1)} %copy-done.1) | data formatting | bytes 163840
Async XLA Ops:
  48.9 1.6 %copy-start.4 = (f32[8,8,320]{2,1,0:T(8,128)S(1)}, f32[8,8,320]{2,1,0:T(8,128)}, u32[]{:S(2)}) copy-start(f32[8,8,320]{2,1,0:T(8,128)} %get-tuple-element.13) | copy-start | bytes 245764
  50.5 0.9 %copy-start.3 = (f32[8,8,320]{2,1,0:T(8,128)S(1)}, f32[8,8,320]{2,1,0:T(8,128)}, u32[]{:S(2)}) copy-start(f32[8,8,320]{2,1,0:T(8,128)} %get-tuple-element.14) | copy-start | bytes 245764
  50.5 1.6 %copy-start.2 = (f32[8,8,320]{2,1,0:T(8,128)S(1)}, f32[8,8,320]{2,1,0:T(8,128)}, u32[]{:S(2)}) copy-start(f32[8,8,320]{2,1,0:T(8,128)} %get-tuple-element.15) | copy-start | bytes 245764
  51.5 1.3 %copy-start = (bf16[4,8,8,320]{3,2,1,0:T(8,128)(2,1)S(1)}, bf16[4,8,8,320]{3,2,1,0:T(8,128)(2,1)}, u32[]{:S(2)}) copy-start(bf16[4,8,8,320]{3,2,1,0:T(8,128)(2,1)} %get-tuple-element.16) | copy-start | bytes 491524
  52.7 1.0 %copy-start.1 = (f32[8,8,320]{2,1,0:T(8,128)S(1)}, f32[8,8,320]{2,1,0:T(8,128)}, u32[]{:S(2)}) copy-start(f32[8,8,320]{2,1,0:T(8,128)} %get-tuple-element.17) | copy-start | bytes 245764
